TPU v7x, 32 devices: a whole 2x2x4 slice. The times are simulated.
32 devices in a mesh: dp: 8 (over y, x, core), tensor: 4 (over z).
Axes of the slice: x: 2, y: 2, z: 4, core: 2. Of those that a mesh axis runs over, the one named last changes fastest.
Arguments:
- norm_input: bfloat16 [16384, 8192], P(('dp', 'tensor')), may hold values from -6 to 6
- key_grad: bfloat16 [16384, 512], P(('dp', 'tensor')), may hold values from -100 to 100
- positions: int32 [16384], P(('dp', 'tensor')), may hold values from 0 to 8191
- norm_gain: bfloat16 [8192], replicated, may hold values from 0.25 to 1.75
- key_weight: bfloat16 [512, 8192], P('dp', 'tensor'), may hold values from -0.0625 to 0.0625
- first_moment: float32 [512, 8192], P('dp', 'tensor'), may hold values from -6 to 6
- second_moment: float32 [512, 8192], P('dp', 'tensor'), may hold values from 0.1 to 4
Outputs:
- input_grad: bfloat16 [16384, 8192], P(('dp', 'tensor'))
- new_weight: bfloat16 [512, 8192], P(None, 'tensor')
- new_first: float32 [512, 8192], P('dp', 'tensor')
- new_second: float32 [512, 8192], P('dp', 'tensor')
All inputs are finite; a program needn't handle non-finite values.
Results may differ from a plain program's by a relative error of at most 0.01.
Values may be sent and summed in bfloat16 or wider, within the bound.
A program may use at most 128 MiB of HBM per device.

v0:
```python
import math

import jax
import jax.numpy as jnp
from jax import lax
from jax.sharding import PartitionSpec as P

D = 8192
KV_HEADS = 4
HEAD = 128


eps_norm = 1e-05
beta_one = 0.9
beta_two = 0.95
learn_rate = 0.0003
decay_rate = 0.1
eps_adam = 1e-08


def unrotate(incoming, positions):
    row_count = incoming.shape[0]
    half_width = HEAD // 2
    frequency = 500000.0 ** (-(2.0 * jnp.arange(half_width, dtype=jnp.float32)) / HEAD)
    angles = positions.astype(jnp.float32)[:, None] * frequency[None, :]
    cosine = jnp.cos(angles)[:, None, :]
    sine_table = jnp.sin(angles)[:, None, :]
    pieces = incoming.astype(jnp.float32).reshape(row_count, KV_HEADS, 2, half_width)
    first_half = pieces[:, :, 0, :]
    second_half = pieces[:, :, 1, :]
    upper_part = first_half * cosine + second_half * sine_table
    lower_part = second_half * cosine - first_half * sine_table
    return (
        jnp.stack([upper_part, lower_part], axis=2)
        .reshape(row_count, KV_HEADS * HEAD)
        .astype(jnp.bfloat16)
    )


def body(norm_input, key_grad, positions, norm_gain, key_weight, first_moment, second_moment):
    local_width = key_weight.shape[1]
    gain_full = norm_gain.astype(jnp.float32)
    gain_local = lax.dynamic_slice_in_dim(
        gain_full, lax.axis_index("tensor") * local_width, local_width, 0
    )
    rotated_back = unrotate(key_grad, positions)
    key_rows = lax.all_gather(rotated_back, "tensor", axis=0, tiled=True)
    upstream_local = jnp.dot(
        key_rows,
        lax.all_gather(key_weight, "dp", axis=0, tiled=True),
        preferred_element_type=jnp.float32,
    )
    received = lax.all_to_all(norm_input, "tensor", split_axis=1, concat_axis=0, tiled=True)
    local_f32 = received.astype(jnp.float32)
    weighted = upstream_local * gain_local
    square_sum, cross_sum = lax.psum(
        (jnp.sum(local_f32 * local_f32, axis=1), jnp.sum(weighted * local_f32, axis=1)), "tensor"
    )
    scale_inv = lax.rsqrt(square_sum / D + eps_norm)[:, None]
    normalized = local_f32 * scale_inv
    feature_normed = (normalized * gain_local).astype(jnp.bfloat16)
    inner = scale_inv * (cross_sum / D)[:, None]
    local_grad = (scale_inv * (weighted - normalized * inner)).astype(jnp.bfloat16)
    input_grad = lax.all_to_all(local_grad, "tensor", split_axis=0, concat_axis=1, tiled=True)
    grad_shard = lax.psum_scatter(
        lax.dot_general(
            key_rows, feature_normed, (((0,), (0,)), ((), ())), preferred_element_type=jnp.float32
        ).astype(jnp.bfloat16),
        "dp",
        scatter_dimension=0,
        tiled=True,
    ).astype(jnp.float32)
    total_square = lax.psum(jnp.sum(grad_shard * grad_shard), ("dp", "tensor"))
    clip_limit = math.sqrt(KV_HEADS * HEAD * D)
    clip_factor = jnp.minimum(1.0, clip_limit / (jnp.sqrt(total_square) + 1e-06))
    clipped = grad_shard * clip_factor
    new_first = beta_one * first_moment + (1.0 - beta_one) * clipped
    new_second = beta_two * second_moment + (1.0 - beta_two) * clipped * clipped
    own_rows = key_weight.astype(jnp.float32)
    updated = (
        own_rows * (1.0 - learn_rate * decay_rate)
        - learn_rate * new_first / (jnp.sqrt(new_second) + eps_adam)
    ).astype(jnp.bfloat16)
    new_weight = lax.all_gather(updated, "dp", axis=0, tiled=True)
    return (input_grad, new_weight, new_first, new_second)


def solution(mesh):
    in_specs = (
        P(("dp", "tensor"), None),
        P(("dp", "tensor"), None),
        P(("dp", "tensor")),
        P(),
        P("dp", "tensor"),
        P("dp", "tensor"),
        P("dp", "tensor"),
    )
    out_specs = (P(("dp", "tensor"), None), P(None, "tensor"), P("dp", "tensor"), P("dp", "tensor"))
    return jax.shard_map(body, mesh=mesh, in_specs=in_specs, out_specs=out_specs, check_vma=False)
```

profile of v0, /device:TPU:0, one launch (start us, length us, event | category | flops | bytes accessed | tf_op | source)
XLA Modules:
  0.0 544.8 jit_solution(5375040626141194060)
XLA Ops:
  7.2 8.4 %copy.20 = bf16[64,4,8,2048]{3,2,0,1:T(8,128)(2,1)} copy(bf16[64,4,8,2048]{3,2,1,0:T(8,128)(2,1)} %bitcast.39) | data formatting | bytes 16777216 | tf_op jit(solution)/shard_map/all_to_all | solution.py:53
  15.6 0.0 copy-start.5
  15.6 0.0 copy-start.2
  15.6 6.5 %all-to-all-start = ((bf16[512,4,2048]{2,0,1:T(8,128)(2,1)}), bf16[512,4,2048]{2,0,1:T(8,128)(2,1)}, u32[]{:S(2)}, u32[]{:S(2)}) async-start(bf16[512,4,2048]{2,0,1:T(8,128)(2,1)} %bitcast.37), calls=%async_computation | async-start | bytes 16777216 | tf_op jit(solution)/shard_map/all_to_all | solution.py:53
  22.1 0.0 all-gather.4.cloned.1.call-start
  22.1 0.0 copy-done.5
  22.1 0.0 copy-done.2
  22.1 0.2 copy.14
  22.3 0.1 convert.11
  22.5 0.5 multiply_cosine_fusion
  23.0 0.2 add_convert_fusion
  23.2 0.8 pad_maximum_fusion
  24.0 0.0 all-gather.4.cloned.1.call-update
  24.1 0.0 all-gather.6.cloned.1.call-start
  24.1 0.7 all-gather.6.cloned.1.call-update
  24.8 0.7 dynamic-slice_convert_fusion
  25.5 214.4 %all-to-all-done = bf16[512,4,2048]{2,0,1:T(8,128)(2,1)} async-done(((bf16[512,4,2048]{2,0,1:T(8,128)(2,1)}), bf16[512,4,2048]{2,0,1:T(8,128)(2,1)}, u32[]{:S(2)}, u32[]{:S(2)}) %all-to-all-start) | async-done | bytes 8388640 | tf_op jit(solution)/shard_map/all_to_all | solution.py:53
  239.9 5.1 fusion.6
  245.0 0.0 all-gather.4.cloned.1.call-done
  245.0 0.0 all-gather.6.cloned.1.call-done
  245.0 15.7 %fusion.7 = (f32[2048]{0:T(1024)S(1)}, f32[2048,2048]{1,0:T(8,128)}) fusion(bf16[512,4,2048]{2,0,1:T(8,128)(2,1)} %all-to-all-done, f32[2048]{0:T(1024)S(1)} %dynamic-slice_convert_fusion, bf16[2048,512]{0,1:T(8,128)(2,1)} %all-gather.4.cloned.1.call-done, bf16[512,2048]{1,0:T(8,128)(2,1)} %all-gather.6.cloned.1.call-done), kind=kOutput, calls=%fused_computation.10 | convolution fusion | flops 4311742464 | bytes 29376512 | tf_op jit(solution)/shard_map/dot_general | solution.py:48
  260.7 16.7 %all-reduce = (f32[2048]{0:T(1024)S(1)}, f32[2048]{0:T(1024)S(1)}) all-reduce(f32[2048]{0:T(1024)S(1)} %get-tuple-element.17, f32[2048]{0:T(1024)S(1)} %bitcast.44), channel_id=1, replica_groups=mesh['dp'=8,'tensor'=4] {'tensor'}, use_global_device_ids=true, to_apply=%region_3.0 | all-reduce | flops 4096 | bytes 32768 | tf_op jit(solution)/shard_map/psum | solution.py:56
  277.5 14.8 %fusion.5 = (bf16[2048,2048]{1,0:T(8,128)(2,1)}, bf16[2048,2048]{1,0:T(8,128)(2,1)}) fusion(bf16[512,4,2048]{2,0,1:T(8,128)(2,1)} %all-to-all-done, f32[2048]{0:T(1024)S(1)} %dynamic-slice_convert_fusion, f32[2048]{0:T(1024)S(1)} %get-tuple-element.13, f32[2048]{0:T(1024)S(1)} %get-tuple-element.14, f32[2048,2048]{1,0:T(8,128)} %get-tuple-element.18), kind=kLoop, calls=%fused_computation.8 | loop fusion | flops 37748736 | bytes 41967616 | tf_op jit(solution)/shard_map/convert_element_type | solution.py:61
  292.3 0.0 copy-start.6
  292.3 5.8 %all-to-all-start.1 = ((bf16[4,512,2048]{2,1,0:T(8,128)(2,1)}), bf16[4,512,2048]{2,1,0:T(8,128)(2,1)}, u32[]{:S(2)}, u32[]{:S(2)}) async-start(bf16[4,512,2048]{2,1,0:T(8,128)(2,1)} %bitcast.38), calls=%async_computation.1 | async-start | bytes 16777216 | tf_op jit(solution)/shard_map/all_to_all | solution.py:64
  298.1 0.2 reduce-scatter.2.cloned.1.call-start
  298.3 0.0 copy-done.6
  298.3 0.0 copy-start.1
  298.3 0.0 copy-start.3
  298.3 0.0 copy-start.4
  298.3 9.1 %convolution_convert_fusion = bf16[512,2048]{1,0:T(8,128)(2,1)} fusion(bf16[2048,512]{0,1:T(8,128)(2,1)S(1)} %copy-done.6, bf16[2048,2048]{1,0:T(8,128)(2,1)} %get-tuple-element.9), kind=kOutput, calls=%fused_computation.12 | convolution fusion | flops 4296015872 | bytes 12582912 | tf_op jit(solution)/shard_map/dot_general | solution.py:66
  307.5 0.0 reduce-scatter.2.cloned.1.call-update
  307.5 0.0 all-gather.8.cloned.1.call-start
  307.6 42.6 %reduce-scatter.2.cloned.1.call-done = bf16[64,2048]{1,0:T(8,128)(2,1)} async-done(((bf16[512,2048]{1,0:T(8,128)(2,1)}), bf16[64,2048]{1,0:T(8,128)(2,1)}) %reduce-scatter.2.cloned.1.call-update) | async-done | bytes 262160 | tf_op jit(solution)/shard_map/reduce_scatter | solution.py:65
  350.2 1.7 fusion.10
  351.9 145.5 %psum.23 = f32[]{:T(128)} all-reduce(f32[]{:T(128)} %fusion.10), channel_id=1, replica_groups=mesh['dp'=8,'tensor'=4] {'dp','tensor'}, use_global_device_ids=true, to_apply=%region_6.0 | all-reduce | flops 1 | bytes 8 | tf_op jit(solution)/shard_map/psum | solution.py:73
  498.1 0.0 copy-done.1
  498.1 0.0 copy-done.3
  498.1 0.0 copy-done.4
  498.1 2.2 subtract_convert_fusion
  500.4 0.0 all-gather.8.cloned.1.call-update
  500.4 27.9 %all-gather.8.cloned.1.call-done = bf16[512,2048]{1,0:T(8,128)(2,1)} async-done(((bf16[64,2048]{1,0:T(8,128)(2,1)}), bf16[512,2048]{1,0:T(8,128)(2,1)}) %all-gather.8.cloned.1.call-update) | async-done | bytes 2097168 | tf_op jit(solution)/shard_map/all_gather | solution.py:84
  528.3 0.0 all-to-all-done.1
  528.3 0.0 copy-start
  528.3 8.6 %copy.17 = bf16[4,64,8,2048]{3,2,0,1:T(8,128)(2,1)} copy(bf16[4,64,8,2048]{3,2,1,0:T(8,128)(2,1)} %bitcast.11) | data formatting | bytes 16777216 | tf_op jit(solution)/shard_map/all_to_all | solution.py:64
  536.9 0.0 copy-done
  536.9 1.3 copy.22
  (4 shorter events, 0.0 us)
Async XLA Ops:
  15.6 6.5 %copy-start.5 = (s32[512]{0:T(512)S(1)}, s32[512]{0:T(512)}, u32[]{:S(2)}) copy-start(s32[512]{0:T(512)} %param.9) | copy-start | bytes 6148
  15.6 6.5 %copy-start.2 = (bf16[512,512]{1,0:T(8,128)(2,1)S(1)}, bf16[512,512]{1,0:T(8,128)(2,1)}, u32[]{:S(2)}) copy-start(bf16[512,512]{1,0:T(8,128)(2,1)} %param.8) | copy-start | bytes 1572868
  15.6 224.3 %all-to-all-start = ((bf16[512,4,2048]{2,0,1:T(8,128)(2,1)}), bf16[512,4,2048]{2,0,1:T(8,128)(2,1)}, u32[]{:S(2)}, u32[]{:S(2)}) async-start(bf16[512,4,2048]{2,0,1:T(8,128)(2,1)} %bitcast.37), calls=%async_computation | async-start | bytes 16777216 | tf_op jit(solution)/shard_map/all_to_all | solution.py:53
  22.1 222.9 %all-gather.4.cloned.1.call-start = ((), (), s32[]{:S(2)}) async-start(), calls=%async_computation.3 | async-start | bytes 2621440 | tf_op jit(solution)/shard_map/all_gather | solution.py:47
  24.1 221.0 %all-gather.6.cloned.1.call-start = ((), (), s32[]{:S(2)}) async-start(), calls=%async_computation.4 | async-start | bytes 2359296 | tf_op jit(solution)/shard_map/all_gather | solution.py:50
  292.3 6.0 %copy-start.6 = (bf16[2048,512]{0,1:T(8,128)(2,1)S(1)}, bf16[2048,512]{0,1:T(8,128)(2,1)}, u32[]{:S(2)}) copy-start(bf16[2048,512]{0,1:T(8,128)(2,1)} %all-gather.4.cloned.1.call-done) | copy-start | bytes 6291460
  292.3 236.0 %all-to-all-start.1 = ((bf16[4,512,2048]{2,1,0:T(8,128)(2,1)}), bf16[4,512,2048]{2,1,0:T(8,128)(2,1)}, u32[]{:S(2)}, u32[]{:S(2)}) async-start(bf16[4,512,2048]{2,1,0:T(8,128)(2,1)} %bitcast.38), calls=%async_computation.1 | async-start | bytes 16777216 | tf_op jit(solution)/shard_map/all_to_all | solution.py:64
  298.1 52.1 %reduce-scatter.2.cloned.1.call-start = ((), (), s32[]{:S(2)}) async-start(), calls=%async_computation.5 | async-start | bytes 2359296 | tf_op jit(solution)/shard_map/reduce_scatter | solution.py:65
  298.3 199.8 %copy-start.1 = (bf16[64,2048]{1,0:T(8,128)(2,1)S(1)}, bf16[64,2048]{1,0:T(8,128)(2,1)}, u32[]{:S(2)}) copy-start(bf16[64,2048]{1,0:T(8,128)(2,1)} %param.11) | copy-start | bytes 786436
  298.3 199.8 %copy-start.3 = (f32[64,2048]{1,0:T(8,128)S(1)}, f32[64,2048]{1,0:T(8,128)}, u32[]{:S(2)}) copy-start(f32[64,2048]{1,0:T(8,128)} %param.12) | copy-start | bytes 1572868
  298.3 199.8 %copy-start.4 = (f32[64,2048]{1,0:T(8,128)S(1)}, f32[64,2048]{1,0:T(8,128)}, u32[]{:S(2)}) copy-start(f32[64,2048]{1,0:T(8,128)} %param.13) | copy-start | bytes 1572868
  307.5 220.8 %all-gather.8.cloned.1.call-start = ((), (), s32[]{:S(2)}) async-start(), calls=%async_computation.6 | async-start | bytes 2359296 | tf_op jit(solution)/shard_map/all_gather | solution.py:84
  528.3 8.6 %copy-start = (bf16[512,2048]{1,0:T(8,128)(2,1)S(1)}, bf16[512,2048]{1,0:T(8,128)(2,1)}, u32[]{:S(2)}) copy-start(bf16[512,2048]{1,0:T(8,128)(2,1)} %all-gather.8.cloned.1.call-done) | copy-start | bytes 6291460
Sparse Core Ops, SparseCore 0:
  25.0 98.1 all-gather.3
  125.1 25.9 all-gather.5
  307.6 42.4 reduce-scatter.1
  500.5 27.7 all-gather.7
where the time goes:
time: 545 us
  waiting for transfers between devices  286 us (52%)
  blocking collectives  162 us (30%)
  other arithmetic  26.2 us (5%)
  matrix products  24.8 us (5%)
  local copies, waits for them, and re-layouts  18.6 us (3%)
  between operations  14.6 us (3%)
  starting transfers between devices  12.5 us (2%)
    all_to_all x1, waiting for transfers between devices, body(): lax.all_to_all(norm_input, 'tensor', split_axis=1, concat_axis=0, tiled=T...  214 us
    psum x1, blocking collectives, body(): total_square = lax.psum(jnp.sum(grad_shard * grad_shard), ('dp', 'tensor'))  146 us
    reduce_scatter x1, waiting for transfers between devices, body(): lax.psum_scatter(lax.dot_general(key_rows, feature_normed, (((0,), (0,)),...  42.6 us
    all_gather x1, waiting for transfers between devices, body(): new_weight = lax.all_gather(updated, 'dp', axis=0, tiled=True)  27.9 us
    psum x1, blocking collectives, body(): lax.psum((jnp.sum(local_f32 * local_f32, axis=1), jnp.sum(weighted * loca...  16.7 us
    dot_general x1, matrix products, body(): jnp.dot(key_rows, lax.all_gather(key_weight, 'dp', axis=0, tiled=True), p...  15.7 us
    convert_element_type x1, other arithmetic, body(): feature_normed = (normalized * gain_local).astype(jnp.bfloat16)  14.8 us
  transfers between devices with their start and end apart: 6, of which 3 were waited for; matrix products, arithmetic and copies ran while one was open for 4% of the time, Pallas kernels for 0%

commit v1 on v0

v1 whole, which is shorter than its diff:
```python
import functools
import math

import jax
import jax.numpy as jnp
from jax import lax
from jax.experimental import pallas as pl
from jax.experimental.pallas import tpu as pltpu
from jax.sharding import PartitionSpec as P

KV_HEADS = 4
HEAD = 128


eps_norm = 1e-05
beta_one = 0.9
beta_two = 0.95
learn_rate = 0.0003
decay_rate = 0.1
eps_adam = 1e-08


def unrotate(incoming, positions):
    row_count = incoming.shape[0]
    half_width = HEAD // 2
    frequency = 500000.0 ** (-(2.0 * jnp.arange(half_width, dtype=jnp.float32)) / HEAD)
    angles = positions.astype(jnp.float32)[:, None] * frequency[None, :]
    cosine = jnp.cos(angles)[:, None, :]
    sine_table = jnp.sin(angles)[:, None, :]
    pieces = incoming.astype(jnp.float32).reshape(row_count, KV_HEADS, 2, half_width)
    first_half = pieces[:, :, 0, :]
    second_half = pieces[:, :, 1, :]
    upper_part = first_half * cosine + second_half * sine_table
    lower_part = second_half * cosine - first_half * sine_table
    return (
        jnp.stack([upper_part, lower_part], axis=2)
        .reshape(row_count, KV_HEADS * HEAD)
        .astype(jnp.bfloat16)
    )


MESH = pl.DeviceIdType.MESH
F32 = jnp.float32
BF16 = jnp.bfloat16


def kernel(
    ndp, nt, x_hbm, kb, kbt, gain, w, m1, m2,
    ig_hbm, nw_hbm, nf, ns,
    x, normed, wf, wg, rcore, rq, zs, rz, gsum, up, sinv, cross, nwb, nsend, nrecv,
    lsem, xsem, osem, a1s, a1r, a2s, a2r, a3s, a3r, cs, cr, qs, qr, zsd, zr, nss, nsr, ws, wr,
):
    nq = ndp // 2
    rows, cols = w.shape
    half = nq * rows
    tokens, width = x.shape
    tile = min(128, tokens)
    ntile = tokens // tile
    cc = min(512, cols)
    dp = lax.axis_index("dp")
    t = lax.axis_index("tensor")
    c = dp % 2
    q = dp // 2
    mate = q * 2 + (1 - c)
    sends = []

    def remote(src, dst, ssem, rsem, dev):
        copy = pltpu.make_async_remote_copy(
            src_ref=src, dst_ref=dst, send_sem=ssem, recv_sem=rsem, device_id=dev, device_id_type=MESH
        )
        copy.start()
        sends.append(copy)
        return copy

    def peer_q(k):
        return ((q + k) % nq) * 2 + c

    def peer_t(i):
        return (t + 1 + i) % nt

    x_in = []
    for k in range(ntile):
        piece = pl.ds(k * tile, tile)
        copy = pltpu.make_async_copy(x_hbm.at[piece], x.at[piece], xsem.at[k])
        copy.start()
        x_in.append(copy)
    my_rows = pl.ds(pl.multiple_of((c * nq + q) * rows, rows), rows)
    own = pltpu.make_async_copy(w, wf.at[t, my_rows], lsem)
    own.start()

    barrier = pltpu.get_barrier_semaphore()
    pl.semaphore_signal(barrier, inc=1, device_id=(mate, t), device_id_type=MESH)
    for k in range(1, nq):
        pl.semaphore_signal(barrier, inc=1, device_id=(peer_q(k), t), device_id_type=MESH)
    for i in range(nt - 1):
        pl.semaphore_signal(barrier, inc=1, device_id=(dp, peer_t(i)), device_id_type=MESH)
    pl.semaphore_wait(barrier, 1 + (nq - 1) + (nt - 1))

    a1 = [remote(w, wf.at[t, my_rows], a1s.at[i], a1r.at[i], (dp, peer_t(i))) for i in range(nt - 1)]

    for k in range(ntile):
        x_in[k].wait()

        @pl.loop(0, tile // 16)
        def _(g):
            r = pl.ds(pl.multiple_of(k * tile + g * 16, 16), 16)
            v = x[r, :].astype(F32)
            s = lax.rsqrt(jnp.sum(v * v, axis=1, keepdims=True) / width + eps_norm)
            sinv[r, :] = jnp.broadcast_to(s, (16, 128))
            normed[r, :] = (v * s * gain[...]).astype(BF16)

    def product(j):
        @pl.loop(0, cols // cc)
        def _(h):
            off = pl.multiple_of(h * cc, cc)
            col = pl.ds(pl.multiple_of(j * cols + h * cc, cc), cc)
            wg[j, :, pl.ds(off, cc)] = jnp.dot(
                kbt[...], normed[:, col], preferred_element_type=F32
            ).astype(BF16)

    mine = pl.multiple_of(c * half, half)
    theirs = pl.multiple_of((1 - c) * half, half)
    core_copies = []
    q_copies = []

    def pair_sum(i):
        j = peer_t(i)
        core_copies[i].wait_recv()

        @pl.loop(0, half // 16)
        def _(g):
            r = pl.ds(pl.multiple_of(mine + g * 16, 16), 16)
            a = wg[j, r, :].astype(F32) + rcore[j, pl.ds(pl.multiple_of(g * 16, 16), 16), :].astype(F32)
            wg[j, r, :] = a.astype(BF16)

        batch = []
        for k in range(1, nq):
            r = pl.ds(pl.multiple_of(mine + ((q + k) % nq) * rows, rows), rows)
            n = i * (nq - 1) + k - 1
            batch.append(remote(wg.at[j, r], rq.at[i, k - 1], qs.at[n], qr.at[n], (peer_q(k), t)))
        q_copies.append(batch)

    for i in range(nt):
        j = peer_t(i)
        product(j)
        core_copies.append(
            remote(wg.at[j, pl.ds(theirs, half)], rcore.at[j], cs.at[i], cr.at[i], (mate, t))
        )
        if i > 0:
            pair_sum(i - 1)
    pair_sum(nt - 1)

    own.wait()
    a2 = []
    for i in range(nt):
        if i > 0:
            a1[i - 1].wait_recv()
        j = (t + nt - i) % nt
        batch = []
        for k in range(1, nq):
            n = i * (nq - 1) + k - 1
            batch.append(
                remote(wf.at[j, my_rows], wf.at[j, my_rows], a2s.at[n], a2r.at[n], (peer_q(k), t))
            )
        a2.append(batch)

    z_copies = []
    for i in range(nt):
        j = peer_t(i)
        for copy in q_copies[i]:
            copy.wait_recv()

        @pl.loop(0, rows // 16)
        def _(g):
            r = pl.ds(pl.multiple_of(g * 16, 16), 16)
            a = wg[j, pl.ds(pl.multiple_of(mine + q * rows + g * 16, 16), 16), :].astype(F32)
            for k in range(nq - 1):
                a = a + rq[i, k, r, :].astype(F32)
            if i < nt - 1:
                zs[i, r, :] = a.astype(BF16)
            else:
                gsum[r, :] = a

        if i < nt - 1:
            z_copies.append(remote(zs.at[i], rz.at[i], zsd.at[i], zr.at[i], (dp, j)))
    for copy in z_copies:
        copy.wait_recv()

    nsend[0] = jnp.zeros((8, 128), F32)

    @pl.loop(0, rows // 16)
    def _(g):
        r = pl.ds(pl.multiple_of(g * 16, 16), 16)
        a = gsum[r, :]
        for i in range(nt - 1):
            a = a + rz[i, r, :].astype(F32)
        gsum[r, :] = a
        a = a * a
        a = a[:8] + a[8:]
        total = a[:, :128]
        for k in range(1, cols // 128):
            total = total + a[:, k * 128 : (k + 1) * 128]
        nsend[0] += total

    copy = remote(nsend.at[0], nrecv.at[0], nss.at[0], nsr.at[0], (mate, t))
    copy.wait_recv()
    nsend[1] = nsend[0] + nrecv[0]
    batch = [
        remote(nsend.at[1], nrecv.at[k], nss.at[k], nsr.at[k], (peer_q(k), t)) for k in range(1, nq)
    ]
    v = nsend[1]
    for k, copy in enumerate(batch):
        copy.wait_recv()
        v = v + nrecv[k + 1]
    nsend[2] = v
    batch = [
        remote(nsend.at[2], nrecv.at[nq + i], nss.at[nq + i], nsr.at[nq + i], (dp, peer_t(i)))
        for i in range(nt - 1)
    ]
    for i, copy in enumerate(batch):
        copy.wait_recv()
        v = v + nrecv[nq + i]
    total_square = jnp.sum(jnp.sum(v, axis=1, keepdims=True), axis=0, keepdims=True)
    limit = math.sqrt(kbt.shape[0] * width)
    clip = jnp.minimum(1.0, limit / (jnp.sqrt(total_square) + 1e-06))
    slot = pl.multiple_of(c * rows, rows)

    @pl.loop(0, rows // 16)
    def _(g):
        r = pl.ds(pl.multiple_of(g * 16, 16), 16)
        clipped = gsum[r, :] * clip
        first = beta_one * m1[r, :] + (1.0 - beta_one) * clipped
        second = beta_two * m2[r, :] + (1.0 - beta_two) * clipped * clipped
        nf[r, :] = first
        ns[r, :] = second
        nwb[q, pl.ds(pl.multiple_of(slot + g * 16, 16), 16), :] = (
            w[r, :].astype(F32) * (1.0 - learn_rate * decay_rate)
            - learn_rate * first / (jnp.sqrt(second) + eps_adam)
        ).astype(BF16)

    part = nwb.at[q, pl.ds(slot, rows)]
    w_copies = [remote(part, part, ws.at[k], wr.at[k], (peer_q(k), t)) for k in range(1, nq)]

    a3 = []
    for i in range(nt):
        for copy in a2[i]:
            copy.wait_recv()
        j = (t + nt - i) % nt
        part = wf.at[j, pl.ds(mine, half)]
        a3.append(remote(part, part, a3s.at[i], a3r.at[i], (mate, t)))
    for copy in a3:
        copy.wait_recv()

    per = cols // cc
    outs = []
    for k in range(ntile):
        piece = pl.ds(k * tile, tile)
        cross[...] = jnp.zeros_like(cross)

        @pl.loop(0, width // cc)
        def _(h):
            col = pl.ds(pl.multiple_of(h * cc, cc), cc)
            u = jnp.dot(
                kb[piece, :],
                wf[h // per, :, pl.ds(pl.multiple_of((h % per) * cc, cc), cc)],
                preferred_element_type=F32,
            ) * gain[:, col]
            up[:, col] = u
            p = u * x[piece, col].astype(F32)
            total = p[:, :128]
            for b in range(1, cc // 128):
                total = total + p[:, b * 128 : (b + 1) * 128]
            cross[...] += total

        @pl.loop(0, tile // 16)
        def _(g):
            l = pl.ds(pl.multiple_of(g * 16, 16), 16)
            r = pl.ds(pl.multiple_of(k * tile + g * 16, 16), 16)
            s = sinv[r, :1]
            inner = s * (jnp.sum(cross[l, :], axis=1, keepdims=True) / width)
            normed[r, :] = (s * (up[l, :] - x[r, :].astype(F32) * s * inner)).astype(BF16)

        copy = pltpu.make_async_copy(normed.at[piece], ig_hbm.at[piece], osem.at[k])
        copy.start()
        outs.append(copy)

    for copy in w_copies:
        copy.wait_recv()
    part = nwb.at[:, pl.ds(slot, rows)]
    last = remote(part, part, ws.at[0], wr.at[0], (mate, t))
    last.wait_recv()
    copy = pltpu.make_async_copy(nwb, nw_hbm, lsem)
    copy.start()
    for copy_out in outs:
        copy_out.wait()
    for sent in sends:
        sent.wait_send()
    copy.wait()


def body(ndp, nt, norm_input, key_grad, positions, norm_gain, key_weight, first_moment, second_moment):
    rows, cols = key_weight.shape
    tokens, width = norm_input.shape
    nq = ndp // 2
    features = ndp * rows
    back = unrotate(key_grad, positions)
    back = back.reshape(tokens, nq, 2, rows).transpose(0, 2, 1, 3).reshape(tokens, features)
    tile = min(128, tokens)
    ntile = tokens // tile
    any_spec = pl.BlockSpec(memory_space=pl.ANY)
    vmem = pl.BlockSpec(memory_space=pltpu.VMEM)
    dma = pltpu.SemaphoreType.DMA
    scratch = [
        pltpu.VMEM((tokens, width), BF16),
        pltpu.VMEM((tokens, width), BF16),
        pltpu.VMEM((nt, features, cols), BF16),
        pltpu.VMEM((nt, features, cols), BF16),
        pltpu.VMEM((nt, nq * rows, cols), BF16),
        pltpu.VMEM((nt, nq - 1, rows, cols), BF16),
        pltpu.VMEM((nt - 1, rows, cols), BF16),
        pltpu.VMEM((nt - 1, rows, cols), BF16),
        pltpu.VMEM((rows, cols), F32),
        pltpu.VMEM((tile, width), F32),
        pltpu.VMEM((tokens, 128), F32),
        pltpu.VMEM((tile, 128), F32),
        pltpu.VMEM((nq, 2 * rows, cols), BF16),
        pltpu.VMEM((3, 8, 128), F32),
        pltpu.VMEM((nq + nt - 1, 8, 128), F32),
        dma, dma((ntile,)), dma((ntile,)),
        dma((nt - 1,)), dma((nt - 1,)),
        dma((nt * (nq - 1),)), dma((nt * (nq - 1),)),
        dma((nt,)), dma((nt,)),
        dma((nt,)), dma((nt,)),
        dma((nt * (nq - 1),)), dma((nt * (nq - 1),)),
        dma((nt - 1,)), dma((nt - 1,)),
        dma((nq + nt - 1,)), dma((nq + nt - 1,)),
        dma((nq,)), dma((nq,)),
    ]
    input_grad, new_weight, new_first, new_second = pl.pallas_call(
        functools.partial(kernel, ndp, nt),
        out_shape=(
            jax.ShapeDtypeStruct((tokens, width), BF16),
            jax.ShapeDtypeStruct((nq, 2 * rows, cols), BF16),
            jax.ShapeDtypeStruct((rows, cols), F32),
            jax.ShapeDtypeStruct((rows, cols), F32),
        ),
        in_specs=[any_spec] + [vmem] * 6,
        out_specs=(any_spec, any_spec, vmem, vmem),
        scratch_shapes=scratch,
        compiler_params=pltpu.CompilerParams(
            collective_id=0, has_side_effects=True, vmem_limit_bytes=62 * 2**20
        ),
    )(
        norm_input, back, back.T, norm_gain.astype(F32)[None, :], key_weight, first_moment, second_moment,
    )
    return (input_grad, new_weight.reshape(features, cols), new_first, new_second)


def solution(mesh):
    in_specs = (
        P(("dp", "tensor"), None),
        P(("dp", "tensor"), None),
        P(("dp", "tensor")),
        P(),
        P("dp", "tensor"),
        P("dp", "tensor"),
        P("dp", "tensor"),
    )
    out_specs = (P(("dp", "tensor"), None), P(None, "tensor"), P("dp", "tensor"), P("dp", "tensor"))
    return jax.shard_map(
        functools.partial(body, mesh.shape["dp"], mesh.shape["tensor"]),
        mesh=mesh, in_specs=in_specs, out_specs=out_specs, check_vma=False,
    )
```

time: 545 us -> 171 us (0.31)
  waiting for transfers between devices: 286 us -> 0 us
  blocking collectives: 162 us -> 0 us
  Pallas kernels: 0 us -> 154 us
  matrix products: 24.8 us -> 0 us
  other arithmetic: 26.2 us -> 2.91 us
  between operations: 14.6 us -> 0.72 us
  starting transfers between devices: 12.5 us -> 0 us
  local copies, waits for them, and re-layouts: 18.6 us -> 13.1 us
    all_to_all x2 -> x0, waiting for transfers between devices: 214 us -> none  [the longest x1 214 us: body(): lax.all_to_all(norm_input, 'tensor', split_axis=1, concat_axis=0, tiled=T...]
    psum x2 -> x0, blocking collectives: 162 us -> none  [the longest x1 146 us: body(): total_square = lax.psum(jnp.sum(grad_shard * grad_shard), ('dp', 'tensor'))]
    pallas_call x0 -> x1, Pallas kernels: none -> 154 us  [body(): pl.pallas_call(functools.partial(kernel, ndp, nt), out_shape=(jax.ShapeDt...]
    reduce_scatter x1 -> x0, waiting for transfers between devices: 42.6 us -> none  [body(): lax.psum_scatter(lax.dot_general(key_rows, feature_normed, (((0,), (0,)),...]
    all_gather x3 -> x0, waiting for transfers between devices: 28 us -> none  [the longest x1 27.9 us: body(): new_weight = lax.all_gather(updated, 'dp', axis=0, tiled=True)]
    dot_general x2 -> x0, matrix products: 24.8 us -> none  [the longest x1 15.7 us: body(): jnp.dot(key_rows, lax.all_gather(key_weight, 'dp', axis=0, tiled=True), p...]
    convert_element_type x3 -> x0, other arithmetic: 17.7 us -> none  [the longest x1 14.8 us: body(): feature_normed = (normalized * gain_local).astype(jnp.bfloat16)]
    all_to_all x2 -> x0, local copies, waits for them, and re-layouts: 17 us -> none  [the longest x1 8.59 us: body(): lax.all_to_all(local_grad, 'tensor', split_axis=0, concat_axis=1, tiled=T...]
  transfers between devices with their start and end apart: 6 -> 0, of which waited for: 3 -> 0; matrix products, arithmetic and copies ran while one was open for 4% -> 0% of each run, Pallas kernels for 0% -> 0%
where the time goes in v1:
time: 171 us
  Pallas kernels  154 us (90%)
  local copies, waits for them, and re-layouts  13.1 us (8%)
  other arithmetic  2.91 us (2%)
    pallas_call x1, Pallas kernels, body(): pl.pallas_call(functools.partial(kernel, ndp, nt), out_shape=(jax.ShapeDt...  154 us
    unnamed x13, local copies, waits for them, and re-layouts  12.1 us

profile of v1, /device:TPU:0, one launch (start us, length us, event | category | flops | bytes accessed | tf_op | source)
XLA Modules:
  0.0 170.5 jit_solution(11073110720546782912)
XLA Ops:
  0.6 0.7 convert_element_type.3
  1.3 1.3 broadcast_in_dim.11
  2.7 0.5 multiply_cosine_fusion
  3.2 1.3 copy.14
  4.5 0.1 convert.10
  4.6 0.2 add_convert_fusion
  4.8 0.1 maximum_bitcast_fusion
  4.9 0.0 copy-start
  4.9 1.0 copy.16.kb
  5.9 0.0 copy-done
  5.9 153.8 %shard_map.102 = (bf16[512,8192]{1,0:T(8,128)(2,1)}, bf16[4,128,2048]{2,1,0:T(8,128)(2,1)}, f32[64,2048]{1,0:T(8,128)}, f32[64,2048]{1,0:T(8,128)}) custom-call(bf16[512,8192]{1,0:T(8,128)(2,1)} %x_hbm.1, bf16[512,512]{1,0:T(8,128)(2,1)} %copy.16.kb, bf16[512,512]{1,0:T(8,128)(2,1)} %bitcast.10, f32[1,8192]{1,0:T(1,128)} %bitcast.13, bf16[64,2048]{1,0:T(8,128)(2,1)} %w.1, ...), custom_call_target="tpu_custom_call" | custom-call | tf_op jit(solution)/shard_map/pallas_call | solution.py:339
  159.7 0.0 copy-start.1
  159.7 0.0 copy-start.3
  159.7 0.0 copy-start.2
  159.7 7.9 %copy.21 = bf16[512,8192]{1,0:T(8,128)(2,1)} copy(bf16[512,8192]{1,0:T(8,128)(2,1)} %get-tuple-element.20) | data formatting | bytes 16777216
  167.6 0.0 copy-done.1
  167.6 1.3 copy.22
  169.0 0.0 copy-done.3
  169.0 0.8 copy.23
  169.8 0.0 copy-done.2
  169.8 0.8 copy.24
  (2 shorter events, 0.0 us)
Async XLA Ops:
  4.9 1.0 copy-start
  159.7 8.0 %copy-start.1 = (bf16[4,128,2048]{2,1,0:T(8,128)(2,1)S(1)}, bf16[4,128,2048]{2,1,0:T(8,128)(2,1)}, u32[]{:S(2)}) copy-start(bf16[4,128,2048]{2,1,0:T(8,128)(2,1)} %get-tuple-element.9) | copy-start | bytes 6291460
  159.7 9.3 %copy-start.3 = (f32[64,2048]{1,0:T(8,128)S(1)}, f32[64,2048]{1,0:T(8,128)}, u32[]{:S(2)}) copy-start(f32[64,2048]{1,0:T(8,128)} %get-tuple-element.22) | copy-start | bytes 1572868
  159.7 10.1 %copy-start.2 = (f32[64,2048]{1,0:T(8,128)S(1)}, f32[64,2048]{1,0:T(8,128)}, u32[]{:S(2)}) copy-start(f32[64,2048]{1,0:T(8,128)} %get-tuple-element.23) | copy-start | bytes 1572868

commit v2 on v1

v2 whole, which is shorter than its diff:
```python
import functools
import math

import jax
import jax.numpy as jnp
from jax import lax
from jax.experimental import pallas as pl
from jax.experimental.pallas import tpu as pltpu
from jax.sharding import PartitionSpec as P

KV_HEADS = 4
HEAD = 128


eps_norm = 1e-05
beta_one = 0.9
beta_two = 0.95
learn_rate = 0.0003
decay_rate = 0.1
eps_adam = 1e-08


def unrotate(incoming, positions):
    row_count = incoming.shape[0]
    half_width = HEAD // 2
    frequency = 500000.0 ** (-(2.0 * jnp.arange(half_width, dtype=jnp.float32)) / HEAD)
    angles = positions.astype(jnp.float32)[:, None] * frequency[None, :]
    cosine = jnp.cos(angles)[:, None, :]
    sine_table = jnp.sin(angles)[:, None, :]
    pieces = incoming.astype(jnp.float32).reshape(row_count, KV_HEADS, 2, half_width)
    first_half = pieces[:, :, 0, :]
    second_half = pieces[:, :, 1, :]
    upper_part = first_half * cosine + second_half * sine_table
    lower_part = second_half * cosine - first_half * sine_table
    return (
        jnp.stack([upper_part, lower_part], axis=2)
        .reshape(row_count, KV_HEADS * HEAD)
        .astype(jnp.bfloat16)
    )


MESH = pl.DeviceIdType.MESH
F32 = jnp.float32
BF16 = jnp.bfloat16


def kernel(
    ndp, nt, nqx, x_hbm, kb, kbt, gain, w, m1, m2,
    ig_hbm, nw_hbm, nf, ns,
    x, normed, wf, wg, rcore, r1a, r1b, r2a, r2b, zs, rz, gsum, sinv, cross, nwb, nsend, nrecv,
    lsem, xsem, osem, a1s, a1r, a2s, a2r, a3s, a3r, b3s, b3r, cs, cr, qs, qr, q2s, q2r,
    zsd, zr, nss, nsr, ws, wr, vs, vr,
):
    nq = ndp // 2
    nqy = nq // nqx
    rows, cols = w.shape
    half = nq * rows
    tokens, width = x.shape
    tile = min(128, tokens)
    ntile = tokens // tile
    cc = min(512, cols)
    hc = cols // 2
    ha = pl.ds(0, hc)
    hb = pl.ds(hc, hc)
    dp = lax.axis_index("dp")
    t = lax.axis_index("tensor")
    c = dp % 2
    q = dp // 2
    qy = q // nqx
    qx = q % nqx
    mate = q * 2 + (1 - c)
    mine = pl.multiple_of(c * half, half)
    theirs = pl.multiple_of((1 - c) * half, half)
    sends = []

    def remote(src, dst, ssem, rsem, dev):
        copy = pltpu.make_async_remote_copy(
            src_ref=src, dst_ref=dst, send_sem=ssem, recv_sem=rsem, device_id=dev, device_id_type=MESH
        )
        copy.start()
        sends.append(copy)
        return copy

    def pos_x(k):
        return (qx + k) % nqx

    def pos_y(k):
        return (qy + k) % nqy

    def dev_x(k):
        return ((qy * nqx + pos_x(k)) * 2 + c, t)

    def dev_y(k):
        return ((pos_y(k) * nqx + qx) * 2 + c, t)

    def slot(yy, xx):
        return pl.ds(pl.multiple_of(mine + (yy * nqx + xx) * rows, rows), rows)

    def peer_t(i):
        return (t + 1 + i) % nt

    x_in = []
    for k in range(ntile):
        piece = pl.ds(k * tile, tile)
        copy = pltpu.make_async_copy(x_hbm.at[piece], x.at[piece], xsem.at[k])
        copy.start()
        x_in.append(copy)
    my_rows = slot(qy, qx)
    own = pltpu.make_async_copy(w, wf.at[t, my_rows], lsem)
    own.start()

    barrier = pltpu.get_barrier_semaphore()
    pl.semaphore_signal(barrier, inc=1, device_id=(mate, t), device_id_type=MESH)
    for k in range(1, nqx):
        pl.semaphore_signal(barrier, inc=1, device_id=dev_x(k), device_id_type=MESH)
    for k in range(1, nqy):
        pl.semaphore_signal(barrier, inc=1, device_id=dev_y(k), device_id_type=MESH)
    for i in range(nt - 1):
        pl.semaphore_signal(barrier, inc=1, device_id=(dp, peer_t(i)), device_id_type=MESH)
    pl.semaphore_wait(barrier, 1 + (nqx - 1) + (nqy - 1) + (nt - 1))

    a1 = [remote(w, wf.at[t, my_rows], a1s.at[i], a1r.at[i], (dp, peer_t(i))) for i in range(nt - 1)]
    na = nqx + nqy - 2
    first_hop = {}
    second_hop = {}

    def block(i):
        return (t + nt - i) % nt

    def gather_first(i):
        j = block(i)
        if i > 0:
            a1[i - 1].wait_recv()
        src = w if i == 0 else wf.at[j, my_rows]
        batch = []
        for k in range(1, nqx):
            n = i * na + k - 1
            batch.append(
                remote(src.at[:, ha], wf.at[j, my_rows, ha], a2s.at[n], a2r.at[n], dev_x(k))
            )
        for k in range(1, nqy):
            n = i * na + nqx - 1 + k - 1
            batch.append(
                remote(src.at[:, hb], wf.at[j, my_rows, hb], a2s.at[n], a2r.at[n], dev_y(k))
            )
        first_hop[i] = batch

    nb = (nqx - 1) * nqy + (nqy - 1) * nqx

    def gather_second(i):
        j = block(i)
        for copy in first_hop[i]:
            copy.wait_recv()
        batch = []
        n = i * nb
        for k in range(1, nqy):
            for xx in range(nqx):
                part = wf.at[j, slot(qy, xx), ha]
                batch.append(remote(part, part, b3s.at[n], b3r.at[n], dev_y(k)))
                n += 1
        for k in range(1, nqx):
            for yy in range(nqy):
                part = wf.at[j, slot(yy, qx), hb]
                batch.append(remote(part, part, b3s.at[n], b3r.at[n], dev_x(k)))
                n += 1
        second_hop[i] = batch

    gather_first(0)
    cross[...] = jnp.zeros_like(cross)

    for k in range(ntile):
        x_in[k].wait()

        @pl.loop(0, tile // 16)
        def _(g):
            r = pl.ds(pl.multiple_of(k * tile + g * 16, 16), 16)
            v = x[r, :].astype(F32)
            s = lax.rsqrt(jnp.sum(v * v, axis=1, keepdims=True) / width + eps_norm)
            sinv[r, :] = jnp.broadcast_to(s, (16, 128))
            normed[r, :] = (v * s * gain[...]).astype(BF16)

    def product(j):
        @pl.loop(0, cols // cc)
        def _(h):
            off = pl.multiple_of(h * cc, cc)
            col = pl.ds(pl.multiple_of(j * cols + h * cc, cc), cc)
            wg[j, :, pl.ds(off, cc)] = jnp.dot(
                kbt[...], normed[:, col], preferred_element_type=F32
            ).astype(BF16)

    core_copies = []
    q_copies = []
    q2_copies = []

    def pair_sum(i):
        j = peer_t(i)
        core_copies[i].wait_recv()

        @pl.loop(0, half // 16)
        def _(g):
            r = pl.ds(pl.multiple_of(mine + g * 16, 16), 16)
            a = wg[j, r, :].astype(F32) + rcore[j, pl.ds(pl.multiple_of(g * 16, 16), 16), :].astype(F32)
            wg[j, r, :] = a.astype(BF16)

        batch = []
        n = i * nb
        for k in range(1, nqx):
            for yy in range(nqy):
                src = wg.at[j, slot(yy, pos_x(k)), ha]
                batch.append(
                    remote(src, r1a.at[i, (k - 1) * nqy + yy], qs.at[n], qr.at[n], dev_x(k))
                )
                n += 1
        for k in range(1, nqy):
            for xx in range(nqx):
                src = wg.at[j, slot(pos_y(k), xx), hb]
                batch.append(
                    remote(src, r1b.at[i, (k - 1) * nqx + xx], qs.at[n], qr.at[n], dev_y(k))
                )
                n += 1
        q_copies.append(batch)

    for i in range(nt):
        j = peer_t(i)
        product(j)
        core_copies.append(
            remote(wg.at[j, pl.ds(theirs, half)], rcore.at[j], cs.at[i], cr.at[i], (mate, t))
        )
        if i > 0:
            pair_sum(i - 1)
    pair_sum(nt - 1)
    own.wait()

    def middle(i):
        j = peer_t(i)
        for copy in q_copies[i]:
            copy.wait_recv()

        @pl.loop(0, rows // 16)
        def _(g):
            l = pl.ds(pl.multiple_of(g * 16, 16), 16)
            for yy in range(nqy):
                r = pl.ds(pl.multiple_of(mine + (yy * nqx + qx) * rows + g * 16, 16), 16)
                a = wg[j, r, ha].astype(F32)
                for k in range(nqx - 1):
                    a = a + r1a[i, k * nqy + yy, l, :].astype(F32)
                wg[j, r, ha] = a.astype(BF16)
            for xx in range(nqx):
                r = pl.ds(pl.multiple_of(mine + (qy * nqx + xx) * rows + g * 16, 16), 16)
                a = wg[j, r, hb].astype(F32)
                for k in range(nqy - 1):
                    a = a + r1b[i, k * nqx + xx, l, :].astype(F32)
                wg[j, r, hb] = a.astype(BF16)

        batch = []
        n = i * na
        for k in range(1, nqy):
            batch.append(
                remote(wg.at[j, slot(pos_y(k), qx), ha], r2a.at[i, k - 1], q2s.at[n], q2r.at[n], dev_y(k))
            )
            n += 1
        for k in range(1, nqx):
            batch.append(
                remote(wg.at[j, slot(qy, pos_x(k)), hb], r2b.at[i, k - 1], q2s.at[n], q2r.at[n], dev_x(k))
            )
            n += 1
        q2_copies.append(batch)

    z_copies = []

    def final(i):
        j = peer_t(i)
        for copy in q2_copies[i]:
            copy.wait_recv()

        @pl.loop(0, rows // 16)
        def _(g):
            r = pl.ds(pl.multiple_of(g * 16, 16), 16)
            m = pl.ds(pl.multiple_of(mine + q * rows + g * 16, 16), 16)
            for part, other, count in ((ha, r2a, nqy - 1), (hb, r2b, nqx - 1)):
                a = wg[j, m, part].astype(F32)
                for k in range(count):
                    a = a + other[i, k, r, :].astype(F32)
                if i < nt - 1:
                    zs[i, r, part] = a.astype(BF16)
                else:
                    gsum[r, part] = a

        if i < nt - 1:
            z_copies.append(remote(zs.at[i], rz.at[i], zsd.at[i], zr.at[i], (dp, j)))

    gather_second(0)
    for i in range(nt):
        middle(i)
        if i > 0:
            gather_first(i)
    for i in range(nt):
        final(i)
        if i > 0:
            gather_second(i)

    a3 = {}

    def gather_third(i):
        for copy in second_hop[i]:
            copy.wait_recv()
        part = wf.at[block(i), pl.ds(mine, half)]
        a3[i] = remote(part, part, a3s.at[i], a3r.at[i], (mate, t))

    uc = min(256, cols)

    def upstream(i):
        j = block(i)
        a3[i].wait_recv()

        @pl.loop(0, cols // uc)
        def _(h):
            off = pl.ds(pl.multiple_of(h * uc, uc), uc)
            col = pl.ds(pl.multiple_of(j * cols + h * uc, uc), uc)
            u = jnp.dot(kb[...], wf[j, :, off], preferred_element_type=F32) * gain[:, col]
            normed[:, col] = u.astype(BF16)
            p = u * x[:, col].astype(F32)
            total = p[:, :128]
            for b in range(1, uc // 128):
                total = total + p[:, b * 128 : (b + 1) * 128]
            cross[...] += total

    gather_third(0)
    upstream(0)
    for copy in z_copies:
        copy.wait_recv()

    nsend[0] = jnp.zeros((8, 128), F32)

    @pl.loop(0, rows // 16)
    def _(g):
        r = pl.ds(pl.multiple_of(g * 16, 16), 16)
        a = gsum[r, :]
        for i in range(nt - 1):
            a = a + rz[i, r, :].astype(F32)
        gsum[r, :] = a
        a = a * a
        a = a[:8] + a[8:]
        total = a[:, :128]
        for k in range(1, cols // 128):
            total = total + a[:, k * 128 : (k + 1) * 128]
        nsend[0] += total

    base = 0
    v = nsend[0]
    groups = (
        [(mate, t)],
        [dev_x(k) for k in range(1, nqx)],
        [dev_y(k) for k in range(1, nqy)],
        [(dp, peer_t(i)) for i in range(nt - 1)],
    )
    for step, devs in enumerate(groups):
        if step > 0:
            nsend[step] = v
        batch = [
            remote(nsend.at[step], nrecv.at[base + n], nss.at[base + n], nsr.at[base + n], dev)
            for n, dev in enumerate(devs)
        ]
        for n, copy in enumerate(batch):
            copy.wait_recv()
            v = v + nrecv[base + n]
        base += len(devs)
    total_square = jnp.sum(jnp.sum(v, axis=1, keepdims=True), axis=0, keepdims=True)
    limit = math.sqrt(kbt.shape[0] * width)
    clip = jnp.minimum(1.0, limit / (jnp.sqrt(total_square) + 1e-06))
    nat = pl.multiple_of(c * rows, rows)

    @pl.loop(0, rows // 16)
    def _(g):
        r = pl.ds(pl.multiple_of(g * 16, 16), 16)
        clipped = gsum[r, :] * clip
        first = beta_one * m1[r, :] + (1.0 - beta_one) * clipped
        second = beta_two * m2[r, :] + (1.0 - beta_two) * clipped * clipped
        nf[r, :] = first
        ns[r, :] = second
        nwb[q, pl.ds(pl.multiple_of(nat + g * 16, 16), 16), :] = (
            w[r, :].astype(F32) * (1.0 - learn_rate * decay_rate)
            - learn_rate * first / (jnp.sqrt(second) + eps_adam)
        ).astype(BF16)

    def piece_of(yy, xx, part):
        return nwb.at[yy * nqx + xx, pl.ds(nat, rows), part]

    w_first = []
    for k in range(1, nqx):
        part = piece_of(qy, qx, ha)
        w_first.append(remote(part, part, ws.at[k - 1], wr.at[k - 1], dev_x(k)))
    for k in range(1, nqy):
        n = nqx - 1 + k - 1
        part = piece_of(qy, qx, hb)
        w_first.append(remote(part, part, ws.at[n], wr.at[n], dev_y(k)))

    for i in range(1, nt):
        gather_third(i)
        upstream(i)

    for copy in w_first:
        copy.wait_recv()
    w_second = []
    for k in range(1, nqy):
        for xx in range(nqx):
            part = piece_of(qy, xx, ha)
            n = len(w_second)
            w_second.append(remote(part, part, vs.at[n], vr.at[n], dev_y(k)))
    for k in range(1, nqx):
        for yy in range(nqy):
            part = piece_of(yy, qx, hb)
            n = len(w_second)
            w_second.append(remote(part, part, vs.at[n], vr.at[n], dev_x(k)))

    outs = []
    for k in range(ntile):
        piece = pl.ds(k * tile, tile)

        @pl.loop(0, tile // 16)
        def _(g):
            r = pl.ds(pl.multiple_of(k * tile + g * 16, 16), 16)
            s = sinv[r, :1]
            inner = s * (jnp.sum(cross[r, :], axis=1, keepdims=True) / width)
            normed[r, :] = (
                s * (normed[r, :].astype(F32) - x[r, :].astype(F32) * s * inner)
            ).astype(BF16)

        copy = pltpu.make_async_copy(normed.at[piece], ig_hbm.at[piece], osem.at[k])
        copy.start()
        outs.append(copy)

    for copy in w_second:
        copy.wait_recv()
    part = nwb.at[:, pl.ds(nat, rows)]
    last = remote(part, part, vs.at[nb], vr.at[nb], (mate, t))
    last.wait_recv()
    copy = pltpu.make_async_copy(nwb, nw_hbm, lsem)
    copy.start()
    for copy_out in outs:
        copy_out.wait()
    for sent in sends:
        sent.wait_send()
    copy.wait()


def body(ndp, nt, norm_input, key_grad, positions, norm_gain, key_weight, first_moment, second_moment):
    rows, cols = key_weight.shape
    tokens, width = norm_input.shape
    nq = ndp // 2
    features = ndp * rows
    back = unrotate(key_grad, positions)
    back = back.reshape(tokens, nq, 2, rows).transpose(0, 2, 1, 3).reshape(tokens, features)
    tile = min(128, tokens)
    ntile = tokens // tile
    any_spec = pl.BlockSpec(memory_space=pl.ANY)
    vmem = pl.BlockSpec(memory_space=pltpu.VMEM)
    dma = pltpu.SemaphoreType.DMA
    nqx = math.isqrt(nq)
    while nq % nqx:
        nqx -= 1
    nqy = nq // nqx
    hc = cols // 2
    na = nqx + nqy - 2
    nb = (nqx - 1) * nqy + (nqy - 1) * nqx
    nn = 1 + na + nt - 1
    scratch = [
        pltpu.VMEM((tokens, width), BF16),
        pltpu.VMEM((tokens, width), BF16),
        pltpu.VMEM((nt, features, cols), BF16),
        pltpu.VMEM((nt, features, cols), BF16),
        pltpu.VMEM((nt, nq * rows, cols), BF16),
        pltpu.VMEM((nt, (nqx - 1) * nqy, rows, hc), BF16),
        pltpu.VMEM((nt, (nqy - 1) * nqx, rows, hc), BF16),
        pltpu.VMEM((nt, nqy - 1, rows, hc), BF16),
        pltpu.VMEM((nt, nqx - 1, rows, hc), BF16),
        pltpu.VMEM((nt - 1, rows, cols), BF16),
        pltpu.VMEM((nt - 1, rows, cols), BF16),
        pltpu.VMEM((rows, cols), F32),
        pltpu.VMEM((tokens, 128), F32),
        pltpu.VMEM((tokens, 128), F32),
        pltpu.VMEM((nq, 2 * rows, cols), BF16),
        pltpu.VMEM((4, 8, 128), F32),
        pltpu.VMEM((nn, 8, 128), F32),
        dma, dma((ntile,)), dma((ntile,)),
    ]
    for count in (nt - 1, nt * na, nt, nt * nb, nt, nt * nb, nt * na, nt - 1, nn, na, nb + 1):
        scratch += [dma((count,)), dma((count,))]
    input_grad, new_weight, new_first, new_second = pl.pallas_call(
        functools.partial(kernel, ndp, nt, nqx),
        out_shape=(
            jax.ShapeDtypeStruct((tokens, width), BF16),
            jax.ShapeDtypeStruct((nq, 2 * rows, cols), BF16),
            jax.ShapeDtypeStruct((rows, cols), F32),
            jax.ShapeDtypeStruct((rows, cols), F32),
        ),
        in_specs=[any_spec] + [vmem] * 6,
        out_specs=(any_spec, any_spec, vmem, vmem),
        scratch_shapes=scratch,
        compiler_params=pltpu.CompilerParams(
            collective_id=0, has_side_effects=True, vmem_limit_bytes=62 * 2**20
        ),
    )(
        norm_input, back, back.T, norm_gain.astype(F32)[None, :], key_weight, first_moment, second_moment,
    )
    return (input_grad, new_weight.reshape(features, cols), new_first, new_second)


def solution(mesh):
    in_specs = (
        P(("dp", "tensor"), None),
        P(("dp", "tensor"), None),
        P(("dp", "tensor")),
        P(),
        P("dp", "tensor"),
        P("dp", "tensor"),
        P("dp", "tensor"),
    )
    out_specs = (P(("dp", "tensor"), None), P(None, "tensor"), P("dp", "tensor"), P("dp", "tensor"))
    return jax.shard_map(
        functools.partial(body, mesh.shape["dp"], mesh.shape["tensor"]),
        mesh=mesh, in_specs=in_specs, out_specs=out_specs, check_vma=False,
    )
```

time: 171 us -> 139 us (0.81)
  Pallas kernels: 154 us -> 122 us
    pallas_call x1, Pallas kernels: 154 us -> 122 us  [body(): pl.pallas_call(functools.partial(kernel, ndp, nt, nqx), out_shape=(jax.Sh...]
where the time goes in v2:
time: 139 us
  Pallas kernels  122 us (88%)
  local copies, waits for them, and re-layouts  13.1 us (9%)
  other arithmetic  2.91 us (2%)
    pallas_call x1, Pallas kernels, body(): pl.pallas_call(functools.partial(kernel, ndp, nt, nqx), out_shape=(jax.Sh...  122 us
    unnamed x13, local copies, waits for them, and re-layouts  12.1 us

profile of v2, /device:TPU:0, one launch (start us, length us, event | category | flops | bytes accessed | tf_op | source)
XLA Modules:
  0.0 139.1 jit_solution(6801877014588810526)
XLA Ops:
  0.6 0.7 convert_element_type.3
  1.3 1.3 broadcast_in_dim.11
  2.7 0.5 multiply_cosine_fusion
  3.2 1.3 copy.14
  4.5 0.1 convert.10
  4.6 0.2 add_convert_fusion
  4.8 0.1 maximum_bitcast_fusion
  4.9 0.0 copy-start
  4.9 1.0 copy.16.kb
  5.9 0.0 copy-done
  5.9 122.4 %shard_map.102 = (bf16[512,8192]{1,0:T(8,128)(2,1)}, bf16[4,128,2048]{2,1,0:T(8,128)(2,1)}, f32[64,2048]{1,0:T(8,128)}, f32[64,2048]{1,0:T(8,128)}) custom-call(bf16[512,8192]{1,0:T(8,128)(2,1)} %x_hbm.1, bf16[512,512]{1,0:T(8,128)(2,1)} %copy.16.kb, bf16[512,512]{1,0:T(8,128)(2,1)} %bitcast.10, f32[1,8192]{1,0:T(1,128)} %bitcast.13, bf16[64,2048]{1,0:T(8,128)(2,1)} %w.1, ...), custom_call_target="tpu_custom_call" | custom-call | tf_op jit(solution)/shard_map/pallas_call | solution.py:489
  128.3 0.0 copy-start.1
  128.3 0.0 copy-start.3
  128.3 0.0 copy-start.2
  128.3 7.9 %copy.21 = bf16[512,8192]{1,0:T(8,128)(2,1)} copy(bf16[512,8192]{1,0:T(8,128)(2,1)} %get-tuple-element.20) | data formatting | bytes 16777216
  136.2 0.0 copy-done.1
  136.2 1.3 copy.22
  137.5 0.0 copy-done.3
  137.5 0.8 copy.23
  138.3 0.0 copy-done.2
  138.3 0.8 copy.24
  (2 shorter events, 0.0 us)
Async XLA Ops:
  4.9 1.0 copy-start
  128.3 8.0 %copy-start.1 = (bf16[4,128,2048]{2,1,0:T(8,128)(2,1)S(1)}, bf16[4,128,2048]{2,1,0:T(8,128)(2,1)}, u32[]{:S(2)}) copy-start(bf16[4,128,2048]{2,1,0:T(8,128)(2,1)} %get-tuple-element.9) | copy-start | bytes 6291460
  128.3 9.3 %copy-start.3 = (f32[64,2048]{1,0:T(8,128)S(1)}, f32[64,2048]{1,0:T(8,128)}, u32[]{:S(2)}) copy-start(f32[64,2048]{1,0:T(8,128)} %get-tuple-element.22) | copy-start | bytes 1572868
  128.3 10.1 %copy-start.2 = (f32[64,2048]{1,0:T(8,128)S(1)}, f32[64,2048]{1,0:T(8,128)}, u32[]{:S(2)}) copy-start(f32[64,2048]{1,0:T(8,128)} %get-tuple-element.23) | copy-start | bytes 1572868

commit v3 on v2

--- a/solution.py
+++ b/solution.py
@@ -179,6 +179,12 @@
             sinv[r, :] = jnp.broadcast_to(s, (16, 128))
             normed[r, :] = (v * s * gain[...]).astype(BF16)
 
+        if k == ntile // 2:
+            own.wait()
+            gather_second(0)
+        if k == ntile - 1:
+            gather_first(1)
+
     def product(j):
         @pl.loop(0, cols // cc)
         def _(h):
@@ -226,10 +232,11 @@
         core_copies.append(
             remote(wg.at[j, pl.ds(theirs, half)], rcore.at[j], cs.at[i], cr.at[i], (mate, t))
         )
+        if i == 1:
+            gather_second(1)
         if i > 0:
             pair_sum(i - 1)
     pair_sum(nt - 1)
-    own.wait()
 
     def middle(i):
         j = peer_t(i)
@@ -289,14 +296,13 @@
         if i < nt - 1:
             z_copies.append(remote(zs.at[i], rz.at[i], zsd.at[i], zr.at[i], (dp, j)))
 
-    gather_second(0)
     for i in range(nt):
         middle(i)
-        if i > 0:
+        if i > 1:
             gather_first(i)
     for i in range(nt):
         final(i)
-        if i > 0:
+        if i > 1:
             gather_second(i)
 
     a3 = {}
@@ -325,8 +331,9 @@
                 total = total + p[:, b * 128 : (b + 1) * 128]
             cross[...] += total
 
-    gather_third(0)
-    upstream(0)
+    for i in range(2):
+        gather_third(i)
+        upstream(i)
     for copy in z_copies:
         copy.wait_recv()
 
@@ -350,9 +357,9 @@
     v = nsend[0]
     groups = (
         [(mate, t)],
+        [(dp, peer_t(i)) for i in range(nt - 1)],
         [dev_x(k) for k in range(1, nqx)],
         [dev_y(k) for k in range(1, nqy)],
-        [(dp, peer_t(i)) for i in range(nt - 1)],
     )
     for step, devs in enumerate(groups):
         if step > 0:
@@ -361,6 +368,10 @@
             remote(nsend.at[step], nrecv.at[base + n], nss.at[base + n], nsr.at[base + n], dev)
             for n, dev in enumerate(devs)
         ]
+        if step == 1:
+            for i in range(2, nt - 1):
+                gather_third(i)
+                upstream(i)
         for n, copy in enumerate(batch):
             copy.wait_recv()
             v = v + nrecv[base + n]
@@ -395,9 +406,8 @@
         part = piece_of(qy, qx, hb)
         w_first.append(remote(part, part, ws.at[n], wr.at[n], dev_y(k)))
 
-    for i in range(1, nt):
-        gather_third(i)
-        upstream(i)
+    gather_third(nt - 1)
+    upstream(nt - 1)
 
     for copy in w_first:
         copy.wait_recv()

time: 139 us -> 134 us (0.964)
  Pallas kernels: 122 us -> 117 us
    pallas_call x1, Pallas kernels: 122 us -> 117 us  [body(): pl.pallas_call(functools.partial(kernel, ndp, nt, nqx), out_shape=(jax.Sh...]
where the time goes in v3:
time: 134 us; the launch traced here: 133 us
  Pallas kernels  117 us (87%)
  local copies, waits for them, and re-layouts  13.1 us (10%)
  other arithmetic  2.91 us (2%)
    pallas_call x1, Pallas kernels, body(): pl.pallas_call(functools.partial(kernel, ndp, nt, nqx), out_shape=(jax.Sh...  117 us
    unnamed x13, local copies, waits for them, and re-layouts  12.1 us

profile of v3, /device:TPU:0, one launch (start us, length us, event | category | flops | bytes accessed | tf_op | source)
XLA Modules:
  0.0 133.4 jit_solution(10907808466328008786)
XLA Ops:
  0.6 0.7 convert_element_type.3
  1.3 1.3 broadcast_in_dim.11
  2.7 0.5 multiply_cosine_fusion
  3.2 1.3 copy.14
  4.5 0.1 convert.10
  4.6 0.2 add_convert_fusion
  4.8 0.1 maximum_bitcast_fusion
  4.9 0.0 copy-start
  4.9 1.0 copy.16.kb
  5.9 0.0 copy-done
  5.9 116.7 %shard_map.102 = (bf16[512,8192]{1,0:T(8,128)(2,1)}, bf16[4,128,2048]{2,1,0:T(8,128)(2,1)}, f32[64,2048]{1,0:T(8,128)}, f32[64,2048]{1,0:T(8,128)}) custom-call(bf16[512,8192]{1,0:T(8,128)(2,1)} %x_hbm.1, bf16[512,512]{1,0:T(8,128)(2,1)} %copy.16.kb, bf16[512,512]{1,0:T(8,128)(2,1)} %bitcast.10, f32[1,8192]{1,0:T(1,128)} %bitcast.13, bf16[64,2048]{1,0:T(8,128)(2,1)} %w.1, ...), custom_call_target="tpu_custom_call" | custom-call | tf_op jit(solution)/shard_map/pallas_call | solution.py:499
  122.6 0.0 copy-start.1
  122.6 0.0 copy-start.3
  122.6 0.0 copy-start.2
  122.6 7.9 %copy.21 = bf16[512,8192]{1,0:T(8,128)(2,1)} copy(bf16[512,8192]{1,0:T(8,128)(2,1)} %get-tuple-element.20) | data formatting | bytes 16777216
  130.5 0.0 copy-done.1
  130.5 1.3 copy.22
  131.8 0.0 copy-done.3
  131.8 0.8 copy.23
  132.6 0.0 copy-done.2
  132.6 0.8 copy.24
  (2 shorter events, 0.0 us)
Async XLA Ops:
  4.9 1.0 copy-start
  122.6 8.0 %copy-start.1 = (bf16[4,128,2048]{2,1,0:T(8,128)(2,1)S(1)}, bf16[4,128,2048]{2,1,0:T(8,128)(2,1)}, u32[]{:S(2)}) copy-start(bf16[4,128,2048]{2,1,0:T(8,128)(2,1)} %get-tuple-element.9) | copy-start | bytes 6291460
  122.6 9.3 %copy-start.3 = (f32[64,2048]{1,0:T(8,128)S(1)}, f32[64,2048]{1,0:T(8,128)}, u32[]{:S(2)}) copy-start(f32[64,2048]{1,0:T(8,128)} %get-tuple-element.22) | copy-start | bytes 1572868
  122.6 10.1 %copy-start.2 = (f32[64,2048]{1,0:T(8,128)S(1)}, f32[64,2048]{1,0:T(8,128)}, u32[]{:S(2)}) copy-start(f32[64,2048]{1,0:T(8,128)} %get-tuple-element.23) | copy-start | bytes 1572868
